TPU v7x, 32 devices: a whole 2x2x4 slice. The times are simulated.
32 devices in a mesh: run: 8 (over z, y), rep: 4 (over x, core).
Axes of the slice: x: 2, y: 2, z: 4, core: 2. Of those that a mesh axis runs over, the one named last changes fastest.
Arguments:
- edge_feats: bfloat16 [4, 16384, 1280], P('rep', 'run'), may hold values from -6 to 6
- edge_grads: bfloat16 [4, 16384, 640], P('rep', 'run'), may hold values from -0.059814453 to 0.059814453
- edge_system: int32 [4, 16384], P('rep', 'run'), may hold values from 0 to 5, as said below
- edge_count: int32 [4, 8], P('rep', 'run'), may hold values from 1025 to 2048
- coef: float32 [4, 6, 32], P('rep'), may hold values from 0.05 to 1
- weights: float32 [32, 1280, 640], P('rep', 'run'), may hold values from -0.15625 to 0.15625
- first_moment: float32 [32, 1280, 640], P('rep', 'run'), may hold values from -6 to 6
- second_moment: float32 [32, 1280, 640], P('rep', 'run'), may hold values from 1 to 10
Outputs:
- new_weights: float32 [32, 1280, 640], P('rep', 'run')
- new_first: float32 [32, 1280, 640], P('rep', 'run')
- new_second: float32 [32, 1280, 640], P('rep', 'run')
- merged_next: bfloat16 [4, 6, 1280, 640], P('rep', None, 'run')
Inputs may be any that keep to these rules, and one draw needn't show every extreme that they name: `edge_system`: along each replica's rows the system never falls; every system number appears; the live rows of one device belong to one or two systems, two on some device in every draw.
All inputs are finite; a program needn't handle non-finite values.
Results may differ from a plain program's by a relative error of at most 0.001.
The roundings to bfloat16 on the way count: a program that leaves them out, or rounds other values in their place, can miss the bound.
Values may be sent and summed in bfloat16 or wider, within the bound.
A program may use at most 128 MiB of HBM per device.

v0:
```python
import jax
import jax.numpy as jnp
from jax import lax
from jax.sharding import PartitionSpec as P


def on_device(
    edge_feats, edge_grads, edge_system, edge_count, coef, weights, first_moment, second_moment
):
    feats = edge_feats[0]
    grads = edge_grads[0]
    system = edge_system[0]
    live_count = edge_count[0, 0]
    group_coef = coef[0]
    nsys = group_coef.shape[0]
    rows = system.shape[0]
    live = jnp.arange(rows) < live_count
    first = system[0]
    last = lax.dynamic_index_in_dim(system, live_count - 1, 0, keepdims=False)
    has_upper = last > first
    empty = jnp.zeros_like(grads)

    def slot_grad(offset):
        keep = live & (system == first + offset)
        right = jnp.where(keep[:, None], grads, empty)
        return lax.dot_general(
            feats, right, (((0,), (0,)), ((), ())), preferred_element_type=jnp.float32
        )

    lower = slot_grad(0)
    upper = lax.cond(has_upper, lambda: slot_grad(1), lambda: jnp.zeros_like(lower))
    stacked = jnp.stack([lower, upper])
    pieces = lax.all_to_all(stacked, "run", split_axis=1, concat_axis=0, tiled=True)
    high_index = jnp.minimum(first + 1, nsys - 1)
    slot_coef = jnp.stack(
        [group_coef[first], group_coef[high_index] * has_upper.astype(jnp.float32)]
    )
    all_coef = lax.all_gather(slot_coef, "run", axis=0, tiled=True)
    mixed = jnp.einsum("ke,kio->eio", all_coef, pieces, precision=lax.Precision.HIGHEST)
    expert_grad = lax.psum_scatter(mixed, "rep", scatter_dimension=0, tiled=True)
    new_first = 0.9 * first_moment + 0.1 * expert_grad
    new_second = 0.999 * second_moment + 0.001 * expert_grad * expert_grad
    corr_first = 1.0 - 0.9**10
    corr_second = 1.0 - 0.999**10
    new_weights = weights - 0.01 * (new_first / corr_first) / (
        jnp.sqrt(new_second / corr_second) + 1e-08
    )
    rounded = lax.optimization_barrier(new_weights.astype(jnp.bfloat16))
    every_expert = lax.all_gather(rounded, "rep", axis=0, tiled=True)
    experts, din_local, dout = every_expert.shape
    flat = every_expert.astype(jnp.float32).reshape(experts, din_local * dout)
    merged = jnp.dot(group_coef, flat, precision=lax.Precision.HIGHEST)
    merged_next = merged.reshape(nsys, din_local, dout).astype(jnp.bfloat16)
    return (new_weights, new_first, new_second, merged_next[None])


def solution(mesh):
    placed = (
        P("rep", "run", None),
        P("rep", "run", None),
        P("rep", "run"),
        P("rep", "run"),
        P("rep", None, None),
        P("rep", "run", None),
        P("rep", "run", None),
        P("rep", "run", None),
    )
    return jax.shard_map(
        on_device,
        mesh=mesh,
        in_specs=placed,
        out_specs=(
            P("rep", "run", None),
            P("rep", "run", None),
            P("rep", "run", None),
            P("rep", None, "run", None),
        ),
        check_vma=False,
    )
```

profile of v0, /device:TPU:0, one launch (start us, length us, event | category | flops | bytes accessed | tf_op | source)
XLA Modules:
  0.0 418.8 jit_solution(7868111956152384483)
XLA Ops:
  7.8 1.3 constant_dynamic-slice_fusion
  9.1 1.4 compare_reduce_fusion.1
  11.8 0.0 copy-start.1
  11.8 8.7 %convolution_bitcast_fusion.1 = f32[1,1280,640]{1,2,0:T(8,128)} fusion(bf16[1,2048,640]{2,1,0:T(8,128)(2,1)} %param.11, pred[2048]{0:T(1024)(128)(4,1)S(1)} %fusion.9, bf16[1,2048,1280]{2,1,0:T(8,128)(2,1)} %param.10), kind=kOutput, calls=%fused_computation.10 | convolution fusion | flops 3356753920 | bytes 11143168 | tf_op jit(solution)/shard_map/dot_general | solution.py:26
  20.5 0.0 copy-done.1
  20.5 0.2 conditional.1
  20.5 0.2 stack.12
  20.8 5.1 %pad_maximum_fusion = f32[2,1280,640]{1,2,0:T(8,128)} fusion(f32[1,1280,640]{1,2,0:T(8,128)S(1)} %get-tuple-element.50, f32[1,1280,640]{1,2,0:T(8,128)} %convolution_bitcast_fusion.1), kind=kLoop, calls=%fused_computation.8 | loop fusion | flops 1638400 | bytes 13107200 | tf_op jit(solution)/shard_map/stack | solution.py:32
  25.8 11.9 %copy.29 = f32[2,1280,640]{2,0,1:T(2,128)} copy(f32[2,1280,640]{1,2,0:T(8,128)} %pad_maximum_fusion) | data formatting | bytes 13107200 | tf_op jit(solution)/shard_map/stack | solution.py:32
  37.8 0.0 copy-start.2
  37.8 15.6 %all-to-all-start = ((f32[2,1280,640]{2,0,1:T(2,128)}), f32[2,1280,640]{2,0,1:T(2,128)}, u32[]{:S(2)}, u32[]{:S(2)}) async-start(f32[2,1280,640]{2,0,1:T(2,128)} %copy.29), calls=%async_computation | async-start | bytes 13107200 | tf_op jit(solution)/shard_map/all_to_all | solution.py:33
  53.4 0.0 reduce-scatter.2.cloned.1.call-start
  56.0 0.0 copy-done.2
  56.1 118.6 %all-gather = f32[8,2,32]{2,1,0:T(2,128)S(1)} all-gather(f32[1,2,32]{2,1,0:T(2,128)S(1)} %maximum_bitcast_fusion), channel_id=1, replica_groups=mesh['run'=8,'rep'=4] {'run'}, dimensions={0}, use_global_device_ids=true | all-gather | bytes 2304 | tf_op jit(solution)/shard_map/all_gather | solution.py:38
  174.7 22.6 %all-to-all-done = f32[2,1280,640]{2,0,1:T(2,128)} async-done(((f32[2,1280,640]{2,0,1:T(2,128)}), f32[2,1280,640]{2,0,1:T(2,128)}, u32[]{:S(2)}, u32[]{:S(2)}) %all-to-all-start) | async-done | bytes 6553632 | tf_op jit(solution)/shard_map/all_to_all | solution.py:33
  197.3 6.0 %copy.30 = f32[2,1280,640]{2,1,0:T(8,128)} copy(f32[2,1280,640]{2,0,1:T(2,128)} %all-to-all-done) | data formatting | bytes 13107200 | tf_op jit(solution)/shard_map/all_to_all | solution.py:33
  203.3 10.6 %copy.31 = f32[8,2,160,640]{3,1,0,2:T(2,128)} copy(f32[8,2,160,640]{3,2,0,1:T(8,128)} %bitcast.53) | data formatting | bytes 13107200 | tf_op jit(solution)/shard_map/all_to_all | solution.py:33
  213.9 8.6 %all_to_all.16 = f32[16,160,640]{2,0,1:T(8,128)} reshape(f32[8,2,160,640]{3,1,0,2:T(2,128)} %copy.31) | data formatting | bytes 13107200 | tf_op jit(solution)/shard_map/all_to_all | solution.py:33
  222.5 14.2 %fusion.20 = f32[32,160,640]{2,0,1:T(8,128)} fusion(f32[16,32,1]{1,0,2:T(8,128)S(1)} %bitcast.56, f32[16,160,640]{2,0,1:T(8,128)} %all_to_all.16), kind=kOutput, calls=%fused_computation.36 | convolution fusion | flops 629145600 | bytes 19662848 | tf_op jit(solution)/shard_map/ke,kio->eio/dot_general | solution.py:39
  236.8 0.0 reduce-scatter.2.cloned.1.call-update
  236.8 0.3 all-gather.3.cloned.1.call-start
  237.1 107.3 %reduce-scatter.2.cloned.1.call-done = f32[8,160,640]{2,0,1:T(8,128)} async-done(((f32[32,160,640]{2,0,1:T(8,128)}), f32[8,160,640]{2,0,1:T(8,128)}) %reduce-scatter.2.cloned.1.call-update) | async-done | bytes 3276816 | tf_op jit(solution)/shard_map/reduce_scatter | solution.py:40
  344.4 12.3 %fusion.17 = (bf16[8,160,640]{2,0,1:T(8,128)(2,1)}, f32[8,160,640]{2,0,1:T(8,128)}, f32[8,160,640]{2,0,1:T(8,128)}, f32[8,160,640]{2,0,1:T(8,128)S(1)}) fusion(f32[8,160,640]{2,1,0:T(8,128)} %param.15, f32[8,160,640]{2,0,1:T(8,128)} %reduce-scatter.2.cloned.1.call-done, f32[8,160,640]{2,1,0:T(8,128)} %param.16, f32[8,160,640]{2,1,0:T(8,128)} %param.17), kind=kLoop, calls=%fused_computation.35 | loop fusion | flops 10649600 | bytes 24576000 | tf_op jit(solution)/shard_map/convert_element_type | solution.py:48
  356.7 0.0 all-gather.3.cloned.1.call-update
  356.8 0.0 copy-start
  356.8 4.4 %copy.35 = f32[8,160,640]{2,1,0:T(8,128)} copy(f32[8,160,640]{2,0,1:T(8,128)} %get-tuple-element.43) | data formatting | bytes 6553600
  361.2 0.0 copy-done
  361.2 2.3 copy.36
  363.5 2.3 copy.37
  365.8 38.9 %all-gather.3.cloned.1.call-done = bf16[32,160,640]{2,0,1:T(8,128)(2,1)} async-done(((bf16[8,160,640]{2,0,1:T(8,128)(2,1)}), bf16[32,160,640]{2,0,1:T(8,128)(2,1)}) %all-gather.3.cloned.1.call-update) | async-done | bytes 6553616 | tf_op jit(solution)/shard_map/all_gather | solution.py:49
  404.7 3.4 copy.39
  408.2 2.7 convolution_convert_fusion
  410.8 1.2 copy.56
  (4 shorter events, 0.0 us)
Async XLA Ops:
  11.8 8.8 %copy-start.1 = (s32[1,2048]{1,0:T(1,128)S(1)}, s32[1,2048]{1,0:T(1,128)}, u32[]{:S(2)}) copy-start(s32[1,2048]{1,0:T(1,128)} %param.12) | copy-start | bytes 24580
  37.8 18.3 %copy-start.2 = (f32[1,6,32]{2,0,1:T(1,128)S(1)}, f32[1,6,32]{2,0,1:T(1,128)}, u32[]{:S(2)}) copy-start(f32[1,6,32]{2,0,1:T(1,128)} %param.14) | copy-start | bytes 2308
  37.8 159.5 %all-to-all-start = ((f32[2,1280,640]{2,0,1:T(2,128)}), f32[2,1280,640]{2,0,1:T(2,128)}, u32[]{:S(2)}, u32[]{:S(2)}) async-start(f32[2,1280,640]{2,0,1:T(2,128)} %copy.29), calls=%async_computation | async-start | bytes 13107200 | tf_op jit(solution)/shard_map/all_to_all | solution.py:33
  53.4 291.0 %reduce-scatter.2.cloned.1.call-start = ((), (), s32[]{:S(2)}) async-start(), calls=%async_computation.2 | async-start | bytes 16384000 | tf_op jit(solution)/shard_map/reduce_scatter | solution.py:40
  236.8 167.9 %all-gather.3.cloned.1.call-start = ((), (), s32[]{:S(2)}) async-start(), calls=%async_computation.3 | async-start | bytes 8192000 | tf_op jit(solution)/shard_map/all_gather | solution.py:49
  356.8 4.4 %copy-start = (f32[8,160,640]{2,0,1:T(8,128)S(1)}, f32[8,160,640]{2,0,1:T(8,128)}, u32[]{:S(2)}) copy-start(f32[8,160,640]{2,0,1:T(8,128)} %get-tuple-element.44) | copy-start | bytes 9830404
Sparse Core Ops, SparseCore 0:
  236.9 107.4 reduce-scatter.1
  356.9 47.7 all-gather.2
where the time goes:
time: 420 us; the launch traced here: 419 us
  waiting for transfers between devices  169 us (40%)
  blocking collectives  119 us (28%)
  local copies, waits for them, and re-layouts  52.3 us (12%)
  matrix products  25.6 us (6%)
  other arithmetic  18.8 us (4%)
  between operations  18.7 us (4%)
  starting transfers between devices  15.9 us (4%)
    all_gather x1, blocking collectives, on_device(): all_coef = lax.all_gather(slot_coef, 'run', axis=0, tiled=True)  119 us
    reduce_scatter x1, waiting for transfers between devices, on_device(): lax.psum_scatter(mixed, 'rep', scatter_dimension=0, tiled=True)  107 us
    all_gather x1, waiting for transfers between devices, on_device(): every_expert = lax.all_gather(rounded, 'rep', axis=0, tiled=True)  38.9 us
    all_to_all x3, local copies, waits for them, and re-layouts, on_device(): lax.all_to_all(stacked, 'run', split_axis=1, concat_axis=0, tiled=True)  25.3 us
    all_to_all x1, waiting for transfers between devices, on_device(): lax.all_to_all(stacked, 'run', split_axis=1, concat_axis=0, tiled=True)  22.6 us
    all_to_all x1, starting transfers between devices, on_device(): lax.all_to_all(stacked, 'run', split_axis=1, concat_axis=0, tiled=True)  15.6 us
    dot_general x1, matrix products, on_device(): jnp.einsum('ke,kio->eio', all_coef, pieces, precision=lax.Precision.HIGHEST)  14.2 us
    convert_element_type x1, other arithmetic, on_device(): rounded = lax.optimization_barrier(new_weights.astype(jnp.bfloat16))  12.3 us
  transfers between devices with their start and end apart: 3, of which 3 were waited for; matrix products, arithmetic and copies ran while one was open for 2% of the time, Pallas kernels for 0%

commit v1 on v0

--- a/solution.py
+++ b/solution.py
@@ -30,7 +30,10 @@
     lower = slot_grad(0)
     upper = lax.cond(has_upper, lambda: slot_grad(1), lambda: jnp.zeros_like(lower))
     stacked = jnp.stack([lower, upper])
-    pieces = lax.all_to_all(stacked, "run", split_axis=1, concat_axis=0, tiled=True)
+    pieces = jnp.concatenate(
+        lax.all_to_all(jnp.stack(jnp.split(stacked, lax.axis_size("run"), axis=1)), "run", 0, 0),
+        axis=0,
+    )
     high_index = jnp.minimum(first + 1, nsys - 1)
     slot_coef = jnp.stack(
         [group_coef[first], group_coef[high_index] * has_upper.astype(jnp.float32)]

time: 420 us -> 401 us (0.955)
  local copies, waits for them, and re-layouts: 52.3 us -> 25.1 us
  other arithmetic: 18.8 us -> 26.2 us
    all_to_all x3 -> x0, local copies, waits for them, and re-layouts: 25.3 us -> none  [on_device(): lax.all_to_all(stacked, 'run', split_axis=1, concat_axis=0, tiled=True)]
    another operation x2 -> x1, local copies, waits for them, and re-layouts: 12.2 us -> 0.21 us  [on_device(): stacked = jnp.stack([lower, upper])]
    unnamed x1 -> x8, other arithmetic: 0.01 us -> 11 us
    another operation x0 -> x1, local copies, waits for them, and re-layouts: none -> 10 us  [on_device(): jnp.stack(jnp.split(stacked, lax.axis_size('run'), axis=1))]
    unnamed x10 -> x12, local copies, waits for them, and re-layouts: 10.2 us -> 10.2 us
where the time goes in v1:
time: 401 us; the launch traced here: 400 us
  waiting for transfers between devices  169 us (42%)
  blocking collectives  119 us (30%)
  matrix products  26.6 us (7%)
  other arithmetic  26.2 us (7%)
  local copies, waits for them, and re-layouts  25.1 us (6%)
  between operations  18.7 us (5%)
  starting transfers between devices  15.7 us (4%)
    all_gather x1, blocking collectives, on_device(): all_coef = lax.all_gather(slot_coef, 'run', axis=0, tiled=True)  119 us
    reduce_scatter x1, waiting for transfers between devices, on_device(): lax.psum_scatter(mixed, 'rep', scatter_dimension=0, tiled=True)  108 us
    all_gather x1, waiting for transfers between devices, on_device(): every_expert = lax.all_gather(rounded, 'rep', axis=0, tiled=True)  38.9 us
    all_to_all x1, waiting for transfers between devices, on_device(): lax.all_to_all(jnp.stack(jnp.split(stacked, lax.axis_size('run'), axis=1)...  22.6 us
    all_to_all x1, starting transfers between devices, on_device(): lax.all_to_all(jnp.stack(jnp.split(stacked, lax.axis_size('run'), axis=1)...  15.6 us
    dot_general x1, matrix products, on_device(): jnp.einsum('ke,kio->eio', all_coef, pieces, precision=lax.Precision.HIGHEST)  15.2 us
    convert_element_type x1, other arithmetic, on_device(): rounded = lax.optimization_barrier(new_weights.astype(jnp.bfloat16))  12.3 us
    unnamed x8, other arithmetic  11 us
  transfers between devices with their start and end apart: 3, of which 3 were waited for; matrix products, arithmetic and copies ran while one was open for 2% of the time, Pallas kernels for 0%

profile of v1, /device:TPU:0, one launch (start us, length us, event | category | flops | bytes accessed | tf_op | source)
XLA Modules:
  0.0 399.9 jit_solution(4693919392894131651)
XLA Ops:
  7.8 1.3 constant_dynamic-slice_fusion
  9.1 1.4 compare_reduce_fusion.1
  11.8 0.0 copy-start.2
  11.8 8.7 %convolution_bitcast_fusion.1 = f32[1,1280,640]{1,2,0:T(8,128)} fusion(bf16[1,2048,640]{2,1,0:T(8,128)(2,1)} %param.11, pred[2048]{0:T(1024)(128)(4,1)S(1)} %fusion.34, bf16[1,2048,1280]{2,1,0:T(8,128)(2,1)} %param.10), kind=kOutput, calls=%fused_computation.25 | convolution fusion | flops 3356753920 | bytes 11143168 | tf_op jit(solution)/shard_map/dot_general | solution.py:26
  20.5 0.0 copy-done.2
  20.5 0.2 conditional.1
  20.5 0.2 stack.30
  20.8 0.0 copy-start
  20.8 2.4 fusion.15
  23.2 0.0 copy-done
  23.2 1.5 fusion.18
  24.6 1.5 fusion.21
  26.1 1.5 fusion.24
  27.6 1.2 fusion.27
  28.7 1.5 fusion.30
  30.2 1.5 fusion.12
  31.8 1.4 fusion.32
  33.2 10.0 %copy.28 = f32[8,2,160,640]{3,2,1,0:T(8,128)} copy(f32[8,2,160,640]{2,3,1,0:T(8,128)} %fusion.32) | data formatting | bytes 13107200 | tf_op jit(solution)/shard_map/stack | solution.py:34
  43.2 0.0 copy-start.3
  43.2 15.6 %all-to-all-start = ((f32[8,2,160,640]{3,2,1,0:T(8,128)}), f32[8,2,160,640]{3,2,1,0:T(8,128)}, u32[]{:S(2)}, u32[]{:S(2)}) async-start(f32[8,2,160,640]{3,2,1,0:T(8,128)} %copy.28), calls=%async_computation | async-start | bytes 13107200 | tf_op jit(solution)/shard_map/all_to_all | solution.py:34
  58.8 0.0 reduce-scatter.2.cloned.1.call-start
  61.5 0.0 copy-done.3
  61.5 118.6 %all-gather = f32[8,2,32]{2,1,0:T(2,128)S(1)} all-gather(f32[1,2,32]{2,1,0:T(2,128)S(1)} %maximum_bitcast_fusion), channel_id=1, replica_groups=mesh['run'=8,'rep'=4] {'run'}, dimensions={0}, use_global_device_ids=true | all-gather | bytes 2304 | tf_op jit(solution)/shard_map/all_gather | solution.py:41
  180.1 22.6 %all-to-all-done = f32[8,2,160,640]{3,2,1,0:T(8,128)} async-done(((f32[8,2,160,640]{3,2,1,0:T(8,128)}), f32[8,2,160,640]{3,2,1,0:T(8,128)}, u32[]{:S(2)}, u32[]{:S(2)}) %all-to-all-start) | async-done | bytes 6553632 | tf_op jit(solution)/shard_map/all_to_all | solution.py:34
  202.7 15.2 %fusion.3 = f32[32,160,640]{2,0,1:T(8,128)} fusion(f32[16,32,1]{1,0,2:T(8,128)S(1)} %bitcast.82, f32[16,160,640]{2,1,0:T(8,128)} %bitcast.23), kind=kOutput, calls=%fused_computation.22 | convolution fusion | flops 629145600 | bytes 19662848 | tf_op jit(solution)/shard_map/ke,kio->eio/dot_general | solution.py:42
  217.9 0.0 reduce-scatter.2.cloned.1.call-update
  217.9 0.0 all-gather.3.cloned.1.call-start
  217.9 107.6 %reduce-scatter.2.cloned.1.call-done = f32[8,160,640]{2,0,1:T(8,128)} async-done(((f32[32,160,640]{2,0,1:T(8,128)}), f32[8,160,640]{2,0,1:T(8,128)}) %reduce-scatter.2.cloned.1.call-update) | async-done | bytes 3276816 | tf_op jit(solution)/shard_map/reduce_scatter | solution.py:43
  325.5 12.3 %fusion.42 = (bf16[8,160,640]{2,0,1:T(8,128)(2,1)}, f32[8,160,640]{2,0,1:T(8,128)}, f32[8,160,640]{2,0,1:T(8,128)}, f32[8,160,640]{2,0,1:T(8,128)S(1)}) fusion(f32[8,160,640]{2,1,0:T(8,128)} %param.15, f32[8,160,640]{2,0,1:T(8,128)} %reduce-scatter.2.cloned.1.call-done, f32[8,160,640]{2,1,0:T(8,128)} %param.16, f32[8,160,640]{2,1,0:T(8,128)} %param.17), kind=kLoop, calls=%fused_computation.74 | loop fusion | flops 10649600 | bytes 24576000 | tf_op jit(solution)/shard_map/convert_element_type | solution.py:51
  337.8 0.0 all-gather.3.cloned.1.call-update
  337.9 0.0 copy-start.1
  337.9 4.4 %copy.33 = f32[8,160,640]{2,1,0:T(8,128)} copy(f32[8,160,640]{2,0,1:T(8,128)} %get-tuple-element.43) | data formatting | bytes 6553600
  342.3 0.0 copy-done.1
  342.3 2.3 copy.34
  344.6 2.3 copy.35
  346.9 38.9 %all-gather.3.cloned.1.call-done = bf16[32,160,640]{2,0,1:T(8,128)(2,1)} async-done(((bf16[8,160,640]{2,0,1:T(8,128)(2,1)}), bf16[32,160,640]{2,0,1:T(8,128)(2,1)}) %all-gather.3.cloned.1.call-update) | async-done | bytes 6553616 | tf_op jit(solution)/shard_map/all_gather | solution.py:52
  385.8 3.4 copy.38
  389.2 2.7 convolution_convert_fusion
  391.9 1.2 copy.57
  (4 shorter events, 0.0 us)
Async XLA Ops:
  11.8 8.8 %copy-start.2 = (s32[1,2048]{1,0:T(1,128)S(1)}, s32[1,2048]{1,0:T(1,128)}, u32[]{:S(2)}) copy-start(s32[1,2048]{1,0:T(1,128)} %param.12) | copy-start | bytes 24580
  20.8 2.4 copy-start
  43.2 18.3 %copy-start.3 = (f32[1,6,32]{2,0,1:T(1,128)S(1)}, f32[1,6,32]{2,0,1:T(1,128)}, u32[]{:S(2)}) copy-start(f32[1,6,32]{2,0,1:T(1,128)} %param.14) | copy-start | bytes 2308
  43.2 159.5 %all-to-all-start = ((f32[8,2,160,640]{3,2,1,0:T(8,128)}), f32[8,2,160,640]{3,2,1,0:T(8,128)}, u32[]{:S(2)}, u32[]{:S(2)}) async-start(f32[8,2,160,640]{3,2,1,0:T(8,128)} %copy.28), calls=%async_computation | async-start | bytes 13107200 | tf_op jit(solution)/shard_map/all_to_all | solution.py:34
  58.8 266.6 %reduce-scatter.2.cloned.1.call-start = ((), (), s32[]{:S(2)}) async-start(), calls=%async_computation.2 | async-start | bytes 16384000 | tf_op jit(solution)/shard_map/reduce_scatter | solution.py:43
  217.9 167.9 %all-gather.3.cloned.1.call-start = ((), (), s32[]{:S(2)}) async-start(), calls=%async_computation.3 | async-start | bytes 8192000 | tf_op jit(solution)/shard_map/all_gather | solution.py:52
  337.9 4.4 %copy-start.1 = (f32[8,160,640]{2,0,1:T(8,128)S(1)}, f32[8,160,640]{2,0,1:T(8,128)}, u32[]{:S(2)}) copy-start(f32[8,160,640]{2,0,1:T(8,128)} %get-tuple-element.44) | copy-start | bytes 9830404
Sparse Core Ops, SparseCore 0:
  218.0 107.4 reduce-scatter.1
  338.0 47.7 all-gather.2
